TPU v7x, 32 devices: a whole 2x2x4 slice. The times are simulated.
32 devices in a mesh: sp: 2 (over x), fsdp: 16 (over z, y, core).
Axes of the slice: x: 2, y: 2, z: 4, core: 2. Of those that a mesh axis runs over, the one named last changes fastest.
Arguments:
- tokens: bfloat16 [16, 1024, 1024], P('fsdp', 'sp'), may hold values from -6 to 6
- segments: int32 [16, 1024], P('fsdp', 'sp'), may hold values from 0 to 7, never falling along the last dimension, each value on 1 to 256 neighbouring positions
- cotangent: bfloat16 [16, 1024, 1024], P('fsdp', 'sp'), may hold values from -6 to 6
- gain_attn: bfloat16 [1024], P('fsdp'), may hold values from 0.5 to 1.5
- w_fac: bfloat16 [1024, 800], P('fsdp'), may hold values from -0.25 to 0.25
- w_out: bfloat16 [1024, 1024], P('fsdp'), may hold values from -0.75 to 0.75
- gain_ffn: bfloat16 [1024], P('fsdp'), may hold values from 0.5 to 1.5
- w_gu: bfloat16 [1024, 5632], P('fsdp'), may hold values from -0.1875 to 0.1875
- w_down: bfloat16 [2816, 1024], P('fsdp'), may hold values from -0.109375 to 0.109375
Outputs:
- out: bfloat16 [16, 1024, 1024], P('fsdp', 'sp')
- grad_tokens: float32 [16, 1024, 1024], P('fsdp', 'sp')
- grad_gain_attn: float32 [1024], P('fsdp')
- grad_w_fac: float32 [1024, 800], P('fsdp')
- grad_w_out: float32 [1024, 1024], P('fsdp')
- grad_gain_ffn: float32 [1024], P('fsdp')
- grad_w_gu: float32 [1024, 5632], P('fsdp')
- grad_w_down: float32 [2816, 1024], P('fsdp')
Inputs may be any that keep to these rules, and one draw needn't show every extreme that they name: `segments`: each row of 1024 numbers never falls and uses all 8 document numbers; a document has at most 256 tokens, and one of each row has exactly that many.
All inputs are finite; a program needn't handle non-finite values.
Results may differ from a plain program's by a relative error of at most 0.023.
Values may be sent and summed in bfloat16 or wider, within the bound.
A program may use at most 192 MiB of HBM per device.

v0:
```python
import functools

import jax
import jax.numpy as jnp
from jax import lax
from jax.experimental import pallas as pl
from jax.experimental.pallas import tpu as pltpu
from jax.sharding import PartitionSpec as P


H = 16
DH = 64
RQ = 6
RK = 2
FF = 2816
LANES = 128
NB = (RQ + 2 * RK) * DH
RANKS = RQ + 2 * RK
MOVED = 1024

EPSILON = 1e-06
NEG = -1e30
F32 = jnp.float32
BF16 = jnp.bfloat16


def rms_norm(values, gain_row):
    factor = lax.rsqrt(jnp.mean(values * values, axis=-1, keepdims=True) + EPSILON)
    return values * factor * gain_row


def swiglu(gate_up):
    return jax.nn.silu(gate_up[:, :FF]) * gate_up[:, FF:]


def product(left, right):
    return jnp.dot(left, right, preferred_element_type=F32)


def weight_grad(left, right):
    return jnp.einsum("ta,tb->ab", left, right, preferred_element_type=F32)


def back_product(grad_rows, weight):
    return jnp.einsum("tb,ab->ta", grad_rows, weight, preferred_element_type=F32)


def dot_nt(a, b):
    return lax.dot_general(a, b, (((1,), (1,)), ((), ())), preferred_element_type=F32)


def dot_tn(a, b):
    return lax.dot_general(a, b, (((0,), (0,)), ((), ())), preferred_element_type=F32)


def band_start(index, block, width):
    return pl.multiple_of(jnp.maximum(index * block - (width - block), 0), LANES)


def band_bias(index, start, seg_col, seg_row, block, width):
    rows = index * block + lax.broadcasted_iota(jnp.int32, (block, width), 0)
    cols = start + lax.broadcasted_iota(jnp.int32, (block, width), 1)
    keep = (seg_col == seg_row) & (cols <= rows)
    return jnp.where(keep, 0.0, NEG)


def half_masks(scale):
    lane = lax.broadcasted_iota(jnp.int32, (1, LANES), 1)
    low = jnp.where(lane < DH, scale, 0.0).astype(BF16)
    high = jnp.where(lane < DH, 0.0, scale).astype(BF16)
    return low, high


def split_pair(values, masks):
    return jnp.concatenate([values * masks[0], values * masks[1]], axis=0)


def attend_forward_kernel(q_ref, k_ref, v_ref, segc_ref, segr_ref, o_ref, *, block, width):
    index = pl.program_id(0)
    start = band_start(index, block, width)
    bias = band_bias(index, start, segc_ref[...], segr_ref[:, pl.ds(start, width)], block, width)
    bias = jnp.concatenate([bias, bias], axis=0)
    masks = half_masks(DH ** (-0.5))
    first = lax.broadcasted_iota(jnp.int32, (block, LANES), 1) < DH
    for pair in range(q_ref.shape[1] // LANES):
        lanes = slice(pair * LANES, (pair + 1) * LANES)
        queries = split_pair(q_ref[:, lanes], masks)
        keys = k_ref[pl.ds(start, width), lanes]
        values = v_ref[pl.ds(start, width), lanes]
        scores = dot_nt(queries, keys) + bias
        exponent = jnp.exp(scores - jnp.max(scores, axis=-1, keepdims=True))
        inverse = 1.0 / jnp.sum(exponent, axis=-1, keepdims=True)
        probs = (exponent * inverse).astype(BF16)
        mixed = product(probs, values)
        o_ref[:, lanes] = jnp.where(first, mixed[:block], mixed[block:]).astype(BF16)


def attend_backward_kernel(
    q_ref, k_ref, v_ref, g_ref, segc_ref, segr_ref, dq_ref, dk_ref, dv_ref, dk_acc, dv_acc,
    *, block, width
):
    index = pl.program_id(0)
    start = band_start(index, block, width)
    scaling = DH ** (-0.5)

    @pl.when(index == 0)
    def _():
        dk_acc[...] = jnp.zeros_like(dk_acc)
        dv_acc[...] = jnp.zeros_like(dv_acc)

    bias = band_bias(index, start, segc_ref[...], segr_ref[:, pl.ds(start, width)], block, width)
    bias = jnp.concatenate([bias, bias], axis=0)
    scale_masks = half_masks(scaling)
    unit_masks = half_masks(1.0)
    first = lax.broadcasted_iota(jnp.int32, (block, LANES), 1) < DH
    window = pl.ds(start, width)
    for pair in range(q_ref.shape[1] // LANES):
        lanes = slice(pair * LANES, (pair + 1) * LANES)
        queries = split_pair(q_ref[:, lanes], scale_masks)
        grads = split_pair(g_ref[:, lanes], unit_masks)
        keys = k_ref[window, lanes]
        values = v_ref[window, lanes]
        scores = dot_nt(queries, keys) + bias
        exponent = jnp.exp(scores - jnp.max(scores, axis=-1, keepdims=True))
        inverse = 1.0 / jnp.sum(exponent, axis=-1, keepdims=True)
        probs = exponent * inverse
        grad_probs = dot_nt(grads, values)
        inner = jnp.sum(probs * grad_probs, axis=-1, keepdims=True)
        grad_scores = (probs * (grad_probs - inner)).astype(BF16)
        grad_q = product(grad_scores, keys) * scaling
        dq_ref[:, lanes] = jnp.where(first, grad_q[:block], grad_q[block:]).astype(BF16)
        dk_acc[window, lanes] += dot_tn(grad_scores, queries)
        dv_acc[window, lanes] += dot_tn(probs.astype(BF16), grads)

    @pl.when(index == pl.num_programs(0) - 1)
    def _():
        dk_ref[...] = dk_acc[...].astype(BF16)
        dv_ref[...] = dv_acc[...].astype(BF16)


def attention_specs(length, columns):
    block = LANES
    width = min(length // 4 + block, length)
    whole = pl.BlockSpec((length, columns), lambda i: (0, 0))
    rows = pl.BlockSpec((block, columns), lambda i: (i, 0))
    seg_col = pl.BlockSpec((block, 1), lambda i: (i, 0))
    seg_row = pl.BlockSpec((1, length), lambda i: (0, 0))
    return block, width, whole, rows, seg_col, seg_row


def attend_forward(queries, keys, values, seg_all):
    length, columns = queries.shape
    block, width, whole, rows, seg_col, seg_row = attention_specs(length, columns)
    work = length * width * columns
    return pl.pallas_call(
        functools.partial(attend_forward_kernel, block=block, width=width),
        grid=(length // block,),
        in_specs=[rows, whole, whole, seg_col, seg_row],
        out_specs=rows,
        out_shape=jax.ShapeDtypeStruct((length, columns), BF16),
        cost_estimate=pl.CostEstimate(
            flops=16 * work, bytes_accessed=8 * length * columns, transcendentals=work // DH
        ),
        name="attend_forward",
    )(queries, keys, values, seg_all.reshape(length, 1), seg_all.reshape(1, length))


def attend_backward(queries, keys, values, grads, seg_all):
    length, columns = queries.shape
    block, width, whole, rows, seg_col, seg_row = attention_specs(length, columns)
    work = length * width * columns
    shape = jax.ShapeDtypeStruct((length, columns), BF16)
    return pl.pallas_call(
        functools.partial(attend_backward_kernel, block=block, width=width),
        grid=(length // block,),
        in_specs=[rows, whole, whole, rows, seg_col, seg_row],
        out_specs=[rows, whole, whole],
        out_shape=[shape, shape, shape],
        scratch_shapes=[pltpu.VMEM((length, columns), F32), pltpu.VMEM((length, columns), F32)],
        cost_estimate=pl.CostEstimate(
            flops=40 * work, bytes_accessed=14 * length * columns, transcendentals=work // DH
        ),
        name="attend_backward",
    )(queries, keys, values, grads, seg_all.reshape(length, 1), seg_all.reshape(1, length))


def expansion(heads):
    rows = lax.broadcasted_iota(jnp.int32, (2 * LANES, RANKS * heads * DH), 0) % LANES
    cols = lax.broadcasted_iota(jnp.int32, (2 * LANES, RANKS * heads * DH), 1)
    rank, head = cols // (heads * DH), (cols % (heads * DH)) // DH
    in_k = heads * RQ + head * RK + rank - RQ
    in_v = heads * (RQ + RK) + head * RK + rank - RQ - RK
    source = jnp.where(
        rank < RQ, head * RQ + rank, jnp.where(rank < RQ + RK, in_k, in_v)
    )
    return (rows == source).astype(BF16)


def high_low(values):
    high = values.astype(BF16)
    return high, (values - high.astype(F32)).astype(BF16)


def doubled(factor, rank, first):
    pair = factor[:, (rank // 2) * LANES : (rank // 2 + 1) * LANES]
    turned = pltpu.roll(pair, DH, 1)
    return jnp.where(first, pair, turned) if rank % 2 == 0 else jnp.where(first, turned, pair)


GROUPS = ((0, RQ), (RQ, RK), (RQ + RK, RK))


def heads_forward_kernel(x_ref, gain_ref, w_ref, e_ref, f_ref, q_ref, k_ref, v_ref):
    normed = rms_norm(x_ref[...].astype(F32), gain_ref[...]).astype(BF16)
    factor = product(normed, w_ref[...])
    f_ref[...] = factor
    spread = jnp.concatenate(high_low(factor[:, NB:]), axis=1)
    rows, columns = q_ref.shape
    first = lax.broadcasted_iota(jnp.int32, (rows, LANES), 1) < DH
    for (base, ranks), out_ref in zip(GROUPS, (q_ref, k_ref, v_ref)):
        total = None
        for rank in range(base, base + ranks):
            left = product(spread, e_ref[:, rank * columns : (rank + 1) * columns])
            right = jnp.concatenate([doubled(factor, rank, first)] * (columns // LANES), axis=1)
            total = left * right if total is None else total + left * right
        out_ref[...] = (total * (1.0 / ranks)).astype(BF16)


def heads_backward_kernel(f_ref, e_ref, dq_ref, dk_ref, dv_ref, g_ref):
    factor = f_ref[...]
    spread = jnp.concatenate(high_low(factor[:, NB:]), axis=1)
    rows, columns = dq_ref.shape
    first = lax.broadcasted_iota(jnp.int32, (rows, LANES), 1) < DH
    left_total = jnp.zeros((rows, LANES), F32)
    folded = []
    for (base, ranks), grad_ref in zip(GROUPS, (dq_ref, dk_ref, dv_ref)):
        grad = grad_ref[...].astype(F32) * (1.0 / ranks)
        for rank in range(base, base + ranks):
            ones = e_ref[:, rank * columns : (rank + 1) * columns]
            weighted = product(spread, ones) * grad
            right_grad = weighted[:, :LANES]
            for chunk in range(1, columns // LANES):
                right_grad = right_grad + weighted[:, chunk * LANES : (chunk + 1) * LANES]
            folded.append(right_grad + pltpu.roll(right_grad, DH, 1))
            right = jnp.concatenate([doubled(factor, rank, first)] * (columns // LANES), axis=1)
            high, low = high_low(grad * right)
            left_total = left_total + dot_nt(high, ones[:LANES]) + dot_nt(low, ones[:LANES])
    for pair in range(RANKS // 2):
        g_ref[:, pair * LANES : (pair + 1) * LANES] = jnp.where(
            first, folded[2 * pair], folded[2 * pair + 1]
        ).astype(BF16)
    g_ref[:, NB:] = left_total.astype(BF16)


HEAD_ROWS = 256


def heads_forward(tokens, gain_row, weights, spreader, columns):
    length, width = tokens.shape
    rows = min(HEAD_ROWS, length)
    block = lambda n: pl.BlockSpec((rows, n), lambda i: (i, 0))
    fixed = lambda a: pl.BlockSpec(a.shape, lambda i: (0, 0))
    head = jax.ShapeDtypeStruct((length, columns), BF16)
    return pl.pallas_call(
        heads_forward_kernel,
        grid=(length // rows,),
        in_specs=[block(width), fixed(gain_row), fixed(weights), fixed(spreader)],
        out_specs=[block(NB + LANES)] + [block(columns)] * 3,
        out_shape=[jax.ShapeDtypeStruct((length, NB + LANES), F32), head, head, head],
        name="heads_forward",
    )(tokens, gain_row, weights, spreader)


def heads_backward(factors, spreader, grad_q, grad_k, grad_v):
    length, columns = grad_q.shape
    rows = min(HEAD_ROWS, length)
    block = lambda n: pl.BlockSpec((rows, n), lambda i: (i, 0))
    return pl.pallas_call(
        heads_backward_kernel,
        grid=(length // rows,),
        in_specs=[
            block(NB + LANES), pl.BlockSpec(spreader.shape, lambda i: (0, 0)),
            block(columns), block(columns), block(columns),
        ],
        out_specs=block(NB + LANES),
        out_shape=jax.ShapeDtypeStruct((length, NB + LANES), BF16),
        name="heads_backward",
    )(factors, spreader, grad_q, grad_k, grad_v)


MESH_ID = pl.DeviceIdType.MESH


def place(count):
    me = lax.axis_index("fsdp")
    line, side, core = me // 4, (me // 2) % 2, me % 2
    return me, line, side, core, count // 4


def spot(line, side, core):
    return (line * 2 + side) * 2 + core


def meet(peers):
    barrier = pltpu.get_barrier_semaphore()
    for peer in peers:
        pl.semaphore_signal(barrier, inc=1, device_id=peer, device_id_type=MESH_ID)
    pl.semaphore_wait(barrier, len(peers))


def halves(columns):
    rank = lax.axis_index("sp")
    half = columns // 2
    own = pl.ds(pl.multiple_of(rank * half, LANES), half)
    other = pl.ds(pl.multiple_of((1 - rank) * half, LANES), half)
    return {"sp": 1 - rank}, own, other


def gather_kernel(x_ref, o_ref, local_sem, send_sem, recv_sem, line_sem, mate_sem, *, count, split):
    me, line, side, core, lines = place(count)
    across = [{"fsdp": spot(lax.rem(line + s, lines), side, core)} for s in range(1, lines)]
    beside, partner = {"fsdp": spot(line, 1 - side, core)}, {"fsdp": spot(line, side, 1 - core)}
    if split:
        mate, span, _ = halves(x_ref.shape[1])
    else:
        mate, span = None, slice(None)
    meet(across + [beside, partner] + ([mate] if split else []))
    sends = []

    def copy(src, dst, slot, sem, peer):
        return pltpu.make_async_remote_copy(
            src_ref=src, dst_ref=dst, send_sem=send_sem.at[slot], recv_sem=sem,
            device_id=peer, device_id_type=MESH_ID,
        )

    def send(src, dst, sem, peer):
        made = copy(src, dst, len(sends), sem, peer)
        made.start()
        sends.append(made)

    def forward(src, shard, peer):
        send(src, o_ref.at[shard], recv_sem.at[shard], peer)

    def arrive(ref, sem):
        copy(ref, ref, 0, sem, partner).wait_recv()

    own = pltpu.make_async_copy(x_ref, o_ref.at[me], local_sem)
    own.start()
    for peer in across:
        send(x_ref.at[:, span], o_ref.at[me, :, span], line_sem.at[me], peer)
    forward(x_ref, me, beside)
    forward(x_ref, me, partner)
    sources = [lax.rem(line + lines - s, lines) for s in range(1, lines)]
    if split:
        for source in sources:
            shard = spot(source, side, core)
            part = o_ref.at[shard, :, span]
            arrive(part, line_sem.at[shard])
            send(part, part, mate_sem.at[shard], mate)
    for source in sources:
        shard = spot(source, side, core)
        arrive(o_ref.at[shard, :, span], (mate_sem if split else line_sem).at[shard])
        forward(o_ref.at[shard], shard, beside)
        forward(o_ref.at[shard], shard, partner)
    for source in [line] + sources:
        shard = spot(source, 1 - side, core)
        arrive(o_ref.at[shard], recv_sem.at[shard])
        forward(o_ref.at[shard], shard, partner)
    for source in [line] + sources:
        for which in (side, 1 - side):
            shard = spot(source, which, 1 - core)
            arrive(o_ref.at[shard], recv_sem.at[shard])
    own.wait()
    for made in sends:
        made.wait_send()


def gather_packed(values, count, shards):
    lines = count // 4
    split = shards == 2
    sems = lambda n: pltpu.SemaphoreType.DMA((n,))
    return pl.pallas_call(
        functools.partial(gather_kernel, count=count, split=split),
        out_shape=jax.ShapeDtypeStruct((count,) + values.shape, values.dtype),
        in_specs=[pl.BlockSpec(memory_space=pltpu.VMEM)],
        out_specs=pl.BlockSpec(memory_space=pltpu.VMEM),
        scratch_shapes=[
            pltpu.SemaphoreType.DMA, sems(5 * lines - 2 if split else 4 * lines - 1),
            sems(count), sems(count), sems(count),
        ],
        compiler_params=pltpu.CompilerParams(collective_id=0, has_side_effects=True),
        name="gather_packed",
    )(values)


def scatter_kernel(
    fac_ref, out_ref, rest_ref, gains_ref, o_ref, part, core_in, side_in, line_in, mine, sp_in, last_in,
    core_send, core_recv, side_send, side_recv, line_send, line_recv, sp_send, sp_recv,
    last_send, last_recv,
    *, count, shards
):
    me, line, side, core, lines = place(count)
    rank = lax.axis_index("sp")
    rows = o_ref.shape[0]
    across = [{"fsdp": spot(lax.rem(line + s, lines), side, core)} for s in range(1, lines)]
    beside, partner = {"fsdp": spot(line, 1 - side, core)}, {"fsdp": spot(line, side, 1 - core)}
    others = [{"sp": lax.rem(rank + s, shards)} for s in range(1, shards)]
    meet(across + [beside, partner] + others)
    started = []

    def copy(src, dst, send_sem, recv_sem, peer):
        return pltpu.make_async_remote_copy(
            src_ref=src, dst_ref=dst, send_sem=send_sem, recv_sem=recv_sem,
            device_id=peer, device_id_type=MESH_ID,
        )

    def send(*args):
        made = copy(*args)
        made.start()
        started.append(made)

    def load(shard):
        begin = pl.multiple_of(shard * rows, rows)
        return jnp.concatenate(
            [ref[pl.ds(begin, rows), :] for ref in (fac_ref, out_ref, rest_ref)]
            + [gains_ref[shard]],
            axis=1,
        )

    def from_core(slot):
        copy(part.at[me], core_in.at[slot], core_send.at[slot], core_recv.at[slot], partner).wait_recv()
        return core_in[slot].astype(F32)

    def from_side(slot):
        copy(part.at[me], side_in.at[slot], side_send.at[slot], side_recv.at[slot], beside).wait_recv()
        return side_in[slot].astype(F32)

    targets = [lax.rem(line + s, lines) for s in range(1, lines)] + [line]
    for which in (1 - side, side):
        for target in targets:
            shard = spot(target, which, 1 - core)
            slot = target * 2 + which
            part[shard] = load(shard)
            send(part.at[shard], core_in.at[slot], core_send.at[slot], core_recv.at[slot], partner)
    for target in targets:
        shard = spot(target, 1 - side, core)
        part[shard] = (load(shard).astype(F32) + from_core(target * 2 + 1 - side)).astype(BF16)
        send(part.at[shard], side_in.at[target], side_send.at[target], side_recv.at[target], beside)

    def whole_sum(target):
        shard = spot(target, side, core)
        return load(shard).astype(F32) + from_core(target * 2 + side) + from_side(target)

    if shards == 2:
        mate, span, rest = halves(o_ref.shape[1])
        for s, target in enumerate(targets):
            shard = spot(target, side, core)
            part[shard] = whole_sum(target).astype(BF16)
            send(part.at[shard, :, rest], sp_in.at[s], sp_send.at[s], sp_recv.at[s], mate)
        for s, target in enumerate(targets):
            shard = spot(target, side, core)
            copy(part.at[me, :, rest], sp_in.at[s], sp_send.at[s], sp_recv.at[s], mate).wait_recv()
            total = part[shard, :, span].astype(F32) + sp_in[s].astype(F32)
            if s < lines - 1:
                mine[s] = total.astype(BF16)
                send(mine.at[s], line_in.at[s], line_send.at[s], line_recv.at[s], across[s])
        for s in range(lines - 1):
            copy(mine.at[s], line_in.at[s], line_send.at[s], line_recv.at[s], across[s]).wait_recv()
            total = total + line_in[s].astype(F32)
        mine[lines - 1] = total.astype(BF16)
        send(mine.at[lines - 1], last_in, last_send, last_recv, mate)
        o_ref[:, span] = mine[lines - 1].astype(F32)
        copy(mine.at[lines - 1], last_in, last_send, last_recv, mate).wait_recv()
        o_ref[:, rest] = last_in[...].astype(F32)
    else:
        for s, target in enumerate(targets):
            total = whole_sum(target)
            if s < lines - 1:
                shard = spot(target, side, core)
                part[shard] = total.astype(BF16)
                send(part.at[shard], line_in.at[s], line_send.at[s], line_recv.at[s], across[s])
        for s in range(lines - 1):
            copy(part.at[me], line_in.at[s], line_send.at[s], line_recv.at[s], across[s]).wait_recv()
            total = total + line_in[s].astype(F32)
        mine[0] = total.astype(BF16)
        for s, peer in enumerate(others):
            send(mine.at[0], sp_in.at[s], sp_send.at[s], sp_recv.at[s], peer)
        total = mine[0].astype(F32)
        for s, peer in enumerate(others):
            copy(mine.at[0], sp_in.at[s], sp_send.at[s], sp_recv.at[s], peer).wait_recv()
            total = total + sp_in[s].astype(F32)
        o_ref[...] = total
    for made in started:
        made.wait_send()


def scatter_packed(grad_fac, grad_out, grad_rest, grad_gains, count, shards):
    rows = grad_fac.shape[0] // count
    columns = sum(a.shape[-1] for a in (grad_fac, grad_out, grad_rest, grad_gains))
    lines = count // 4
    split = shards == 2
    span = columns // 2 if split else columns
    passes = lines if split else shards - 1
    buffer = lambda n: pltpu.VMEM((n, rows, columns), BF16)
    narrow = lambda n: pltpu.VMEM((n, rows, span), BF16)
    sems = lambda n: pltpu.SemaphoreType.DMA((n,))
    return pl.pallas_call(
        functools.partial(scatter_kernel, count=count, shards=shards),
        out_shape=jax.ShapeDtypeStruct((rows, columns), F32),
        in_specs=[pl.BlockSpec(memory_space=pltpu.VMEM)] * 4,
        out_specs=pl.BlockSpec(memory_space=pltpu.VMEM),
        scratch_shapes=[
            buffer(count), buffer(2 * lines), buffer(lines), narrow(lines - 1),
            narrow(lines if split else 1), narrow(passes), pltpu.VMEM((rows, span), BF16),
            sems(2 * lines), sems(2 * lines), sems(lines), sems(lines),
            sems(lines - 1), sems(lines - 1), sems(passes), sems(passes),
            pltpu.SemaphoreType.DMA, pltpu.SemaphoreType.DMA,
        ],
        compiler_params=pltpu.CompilerParams(collective_id=1, has_side_effects=True),
        name="scatter_packed",
    )(grad_fac, grad_out, grad_rest, grad_gains)


def gather_shards(values, shards):
    me = lax.axis_index("sp")
    rows = values.shape[0]
    full = jnp.zeros((rows * shards,) + values.shape[1:], values.dtype)
    zeros = (0,) * (values.ndim - 1)
    full = lax.dynamic_update_slice(full, values, (me * rows,) + zeros)
    for shift in range(1, shards):
        part = lax.ppermute(values, "sp", [(i, (i + shift) % shards) for i in range(shards)])
        full = lax.dynamic_update_slice(full, part, (((me - shift) % shards) * rows,) + zeros)
    return full


def sum_shards(values, shards):
    if shards == 2:
        other = lax.ppermute(values, "sp", [(0, 1), (1, 0)])
        return values.astype(F32) + other.astype(F32)
    return lax.psum(values, "sp").astype(F32)


def arrange_factor(w, shards):
    heads = H // shards
    spans = ((0, RQ), (H * RQ, RK), (H * (RQ + RK), RK))
    parts = [w[:, H * RANKS :]]
    for device in range(shards):
        own = [
            w[:, base + device * heads * r : base + (device + 1) * heads * r] for base, r in spans
        ]
        parts.append(jnp.pad(jnp.concatenate(own, axis=1), ((0, 0), (0, LANES - heads * RANKS))))
    return jnp.concatenate(parts, axis=1)


def restore_factor(g, shards):
    heads = H // shards
    spans = ((0, RQ), (heads * RQ, RK), (heads * (RQ + RK), RK))
    parts = []
    for base, r in spans:
        for device in range(shards):
            begin = NB + device * LANES + base
            parts.append(g[:, begin : begin + heads * r])
    parts.append(g[:, :NB])
    return jnp.concatenate(parts, axis=1)


def local(tokens, segments, cotangent, gain_attn, w_fac, w_out, gain_ffn, w_gu, w_down, shards, count):
    me = lax.axis_index("sp")
    features = tokens.shape[2]
    heads = H // shards
    columns = heads * DH
    fac_columns = NB + shards * LANES
    own_rows = w_fac.shape[0]

    gains = jnp.concatenate([gain_attn, gain_ffn])[None]
    gains = jnp.pad(gains, ((0, own_rows - 1), (0, LANES - 2 * own_rows)))
    packed = jnp.concatenate([arrange_factor(w_fac, shards), w_out, gains], axis=1)
    packed = gather_packed(packed, count, shards)
    gu_full = lax.all_gather(w_gu, "fsdp", axis=0, tiled=True)
    down_full = lax.all_gather(w_down, "fsdp", axis=0, tiled=True)
    gains = packed[:, 0, fac_columns + features :].astype(F32)
    gain_one = gains[:, :own_rows].reshape(1, features)
    gain_two = gains[:, own_rows : 2 * own_rows].reshape(1, features)
    packed = packed.reshape(features, packed.shape[2])
    fac_full = packed[:, :fac_columns]
    out_full = packed[:, fac_columns : fac_columns + features]

    tokens_all = gather_shards(tokens[0], shards)
    seg_all = gather_shards(segments[0], shards)
    own_left = lax.dynamic_slice_in_dim(fac_full, NB + me * LANES, LANES, 1)
    own_weights = jnp.concatenate([fac_full[:, :NB], own_left], axis=1)
    spreader = expansion(heads)
    factors, query_heads, key_heads, value_heads = heads_forward(
        tokens_all, gain_one, own_weights, spreader, columns
    )
    mixed_heads = attend_forward(query_heads, key_heads, value_heads, seg_all)
    mixed_tokens = lax.all_to_all(mixed_heads, "sp", split_axis=0, concat_axis=1, tiled=True)

    inputs = tokens[0].astype(F32)
    token_count = inputs.shape[0]
    hidden_in = inputs + product(mixed_tokens, out_full)
    normed_two = rms_norm(hidden_in, gain_two).astype(BF16)
    gate_up = product(normed_two, gu_full)
    activated = swiglu(gate_up).astype(BF16)
    gate_up, activated = lax.optimization_barrier((gate_up, activated))
    grad_out = cotangent[0].astype(F32)
    grad_low = cotangent[0]
    grad_down = weight_grad(activated, grad_low).astype(BF16)
    grad_down = lax.psum_scatter(grad_down, "fsdp", scatter_dimension=0, tiled=True)

    result = hidden_in + product(activated, down_full)
    output = result.astype(BF16)[None]

    grad_act = back_product(grad_low, down_full)
    _, pull_ffn = jax.vjp(swiglu, gate_up)
    grad_gate_up = pull_ffn(grad_act)[0].astype(BF16)
    grad_normed_two = back_product(grad_gate_up, gu_full)
    _, pull_two = jax.vjp(rms_norm, hidden_in, gain_two)
    grad_from_norm, grad_gain_two = pull_two(grad_normed_two)
    grad_hidden = grad_out + grad_from_norm
    grad_branch = grad_hidden.astype(BF16)
    grad_mixed = back_product(grad_branch, out_full).astype(BF16)
    grad_gate_up, grad_mixed = lax.optimization_barrier((grad_gate_up, grad_mixed))
    kept = grad_gate_up.shape[1] - MOVED
    grad_gu = weight_grad(normed_two, grad_gate_up[:, :kept]).astype(BF16)
    grad_gu = lax.psum_scatter(grad_gu, "fsdp", scatter_dimension=0, tiled=True)
    grad_heads = lax.all_to_all(grad_mixed, "sp", split_axis=1, concat_axis=0, tiled=True)
    grad_q, grad_k, grad_v = attend_backward(
        query_heads, key_heads, value_heads, grad_heads, seg_all
    )
    grad_parts = heads_backward(factors, spreader, grad_q, grad_k, grad_v)
    grad_gate_up, grad_branch, grad_parts = lax.optimization_barrier(
        (grad_gate_up, grad_branch, grad_parts)
    )
    grad_rest = weight_grad(normed_two, grad_gate_up[:, kept:]).astype(BF16)
    grad_wout = weight_grad(mixed_tokens, grad_branch)
    grad_parts = lax.all_to_all(
        grad_parts.reshape(shards, token_count, NB + LANES), "sp", split_axis=0, concat_axis=0
    )
    grad_right = jnp.sum(grad_parts[:, :, :NB].astype(F32), axis=0).astype(BF16)
    grad_factor = jnp.concatenate(
        [grad_right] + [grad_parts[device, :, NB:] for device in range(shards)], axis=1
    )
    normed_one = rms_norm(inputs, gain_one).astype(BF16)
    grad_fac = weight_grad(normed_one, grad_factor)
    grad_normed_one = back_product(grad_factor, fac_full)
    _, pull_one = jax.vjp(rms_norm, inputs, gain_one)
    grad_in_norm, grad_gain_one = pull_one(grad_normed_one)
    grad_tokens = (grad_hidden + grad_in_norm).reshape(1, token_count, features)

    grad_gains = jnp.concatenate(
        [grad_gain_one.reshape(count, own_rows), grad_gain_two.reshape(count, own_rows)], axis=1
    )
    grad_gains = jnp.pad(
        grad_gains[:, None], ((0, 0), (0, own_rows - 1), (0, LANES - 2 * own_rows))
    )
    grad_packed = scatter_packed(
        grad_fac.astype(BF16), grad_wout.astype(BF16), grad_rest, grad_gains.astype(BF16),
        count, shards,
    )
    grad_down = sum_shards(grad_down, shards)
    grad_gu = sum_shards(grad_gu, shards)
    tail = fac_columns + features
    gain_row = grad_packed[0, tail + MOVED :]
    grad_gu = jnp.concatenate([grad_gu, grad_packed[:, tail : tail + MOVED]], axis=1)
    return (
        output,
        grad_tokens,
        gain_row[:own_rows],
        restore_factor(grad_packed[:, :fac_columns], shards),
        grad_packed[:, fac_columns : fac_columns + features],
        gain_row[own_rows : 2 * own_rows],
        grad_gu,
        grad_down,
    )


def solution(mesh):
    in_specs = (
        P("fsdp", "sp", None),
        P("fsdp", "sp"),
        P("fsdp", "sp", None),
        P("fsdp"),
        P("fsdp", None),
        P("fsdp", None),
        P("fsdp"),
        P("fsdp", None),
        P("fsdp", None),
    )
    out_specs = (
        P("fsdp", "sp", None),
        P("fsdp", "sp", None),
        P("fsdp"),
        P("fsdp", None),
        P("fsdp", None),
        P("fsdp"),
        P("fsdp", None),
        P("fsdp", None),
    )

    def body(*args):
        return local(*args, shards=mesh.shape["sp"], count=mesh.shape["fsdp"])

    return jax.shard_map(body, mesh=mesh, in_specs=in_specs, out_specs=out_specs, check_vma=False)
```

profile of v0, /device:TPU:12, one launch (start us, length us, event | category | flops | bytes accessed | tf_op | source)
XLA Modules:
  0.0 446.1 jit_solution(8889016495577950137)
XLA Ops:
  16.1 44.7 %gather_packed.1 = bf16[16,64,2048]{2,1,0:T(8,128)(2,1)} custom-call(bf16[64,2048]{1,0:T(8,128)(2,1)} %copy-done.15), custom_call_target="tpu_custom_call" | custom-call | tf_op jit(solution)/shard_map/gather_packed/pallas_call | solution.py:382
  75.4 10.7 %heads_forward.1 = (f32[1024,768]{1,0:T(8,128)}, bf16[1024,512]{1,0:T(8,128)(2,1)}, bf16[1024,512]{1,0:T(8,128)(2,1)}, bf16[1024,512]{1,0:T(8,128)(2,1)}) custom-call(bf16[1024,1024]{1,0:T(8,128)(2,1)} %copy-done.4, f32[1,1024]{1,0:T(1,128)} %reshape.89.gain_ref, bf16[1024,768]{1,0:T(8,128)(2,1)} %pad_maximum_fusion.w_ref, bf16[256,5120]{1,0:T(8,128)(2,1)} %fusion.13.e_ref), custom_call_target="tpu_custom_call" | custom-call | tf_op jit(solution)/shard_map/heads_forward/pallas_call | solution.py:264
  86.1 16.9 %attend_forward.1 = bf16[1024,512]{1,0:T(8,128)(2,1)} custom-call(bf16[1024,512]{1,0:T(8,128)(2,1)} %get-tuple-element.22.q_ref, bf16[1024,512]{1,0:T(8,128)(2,1)} %get-tuple-element.23.k_ref, bf16[1024,512]{1,0:T(8,128)(2,1)} %get-tuple-element.24.v_ref, s32[1024,1]{1,0:T(8,128)} %copy.18.segc_ref, s32[1,1024]{1,0:T(1,128)} %bitcast.86), custom_call_target="tpu_custom_call" | custom-call | flops 3221225472 | bytes 4194304 | tf_op jit(solution)/shard_map/attend_forward/pallas_call | solution.py:155
  109.3 13.9 %all-to-all-done = bf16[2,512,512]{1,2,0:T(8,128)(2,1)S(1)} async-done(((bf16[2,512,512]{1,2,0:T(8,128)(2,1)}), bf16[2,512,512]{1,2,0:T(8,128)(2,1)S(1)}, u32[]{:S(2)}, u32[]{:S(2)}) %all-to-all-start) | async-done | bytes 1048608 | tf_op jit(solution)/shard_map/all_to_all | solution.py:597
  128.7 9.3 %fusion.74 = f32[512,5632]{1,0:T(8,128)S(1)} fusion(bf16[512,1024]{1,0:T(8,128)(2,1)} %multiply_convert_fusion, bf16[1024,5632]{1,0:T(8,128)(2,1)} %all-gather.3.cloned.1.call-done), kind=kOutput, calls=%fused_computation.134 | convolution fusion | flops 5905580032 | bytes 24117248 | tf_op jit(solution)/shard_map/dot_general | solution.py:37
  143.8 5.0 %convolution_convert_fusion.1 = bf16[2816,1024]{1,0:T(8,128)(2,1)} fusion(bf16[512,2816]{1,0:T(8,128)(2,1)S(1)} %fusion.2, bf16[1,512,1024]{2,1,0:T(8,128)(2,1)S(1)} %copy-done.6), kind=kOutput, calls=%fused_computation.21 | convolution fusion | flops 2955673600 | bytes 9699328 | tf_op jit(solution)/shard_map/ta,tb->ab/dot_general | solution.py:41
  149.4 23.9 %all-gather.5.cloned.1.call-done = bf16[2816,1024]{1,0:T(8,128)(2,1)} async-done(((bf16[176,1024]{1,0:T(8,128)(2,1)}), bf16[2816,1024]{1,0:T(8,128)(2,1)}) %all-gather.5.cloned.1.call-update) | async-done | bytes 5767184 | tf_op jit(solution)/shard_map/all_gather | solution.py:580
  173.2 12.3 %multiply_multiply_fusion = (f32[512,2816]{1,0:T(8,128)}, f32[512,2816]{1,0:T(8,128)}) fusion(f32[512,5632]{1,0:T(8,128)} %copy-done.1, bf16[2816,1024]{1,0:T(8,128)(2,1)} %all-gather.5.cloned.1.call-done, bf16[1,512,1024]{2,1,0:T(8,128)(2,1)} %param.11), kind=kOutput, calls=%fused_computation.19 | convolution fusion | flops 2970091520 | bytes 29884416 | tf_op jit(solution)/shard_map/tb,ab->ta/dot_general | solution.py:45
  185.5 8.2 %add_convert_fusion = bf16[512,5632]{1,0:T(8,128)(2,1)} fusion(f32[512,2816]{1,0:T(8,128)} %get-tuple-element.41, f32[512,2816]{1,0:T(8,128)} %get-tuple-element.40), kind=kLoop, calls=%fused_computation.9 | loop fusion | flops 5767168 | bytes 17301504 | tf_op jit(solution)/shard_map/convert_element_type | solution.py:616
  193.7 11.7 %multiply_reduce_fusion = (bf16[1024]{0:T(1024)(128)(2,1)S(1)}, f32[512]{0:T(512)S(1)}, f32[512,1024]{1,0:T(8,128)S(1)}) fusion(f32[512,1024]{1,0:T(8,128)S(1)} %get-tuple-element.63, f32[512]{0:T(512)S(1)} %fusion.60, f32[1024]{0:T(1024)S(1)} %mul.183, bf16[512,5632]{1,0:T(8,128)(2,1)} %add_convert_fusion, bf16[1024,5632]{1,0:T(8,128)(2,1)} %all-gather.3.cloned.1.call-done), kind=kOutput, calls=%fused_computation.50 | convolution fusion | flops 5908724224 | bytes 21506048 | tf_op jit(solution)/shard_map/tb,ab->ta/dot_general | solution.py:45
  211.5 7.6 %convolution_convert_fusion = bf16[1024,4608]{1,0:T(8,128)(2,1)} fusion(bf16[512,1024]{1,0:T(8,128)(2,1)S(1)} %copy-done.10, bf16[512,5632]{1,0:T(8,128)(2,1)S(1)} %bitcast.78), kind=kOutput, calls=%fused_computation.10 | convolution fusion | flops 4836556800 | bytes 15204352 | tf_op jit(solution)/shard_map/ta,tb->ab/dot_general | solution.py:41
  221.5 4.6 %all-to-all-start.1 = ((bf16[512,2,512]{2,0,1:T(8,128)(2,1)}), bf16[512,2,512]{2,0,1:T(8,128)(2,1)}, u32[]{:S(2)}, u32[]{:S(2)}) async-start(bf16[512,2,512]{2,0,1:T(8,128)(2,1)} %bitcast.79), calls=%async_computation.1 | async-start | bytes 2097152 | tf_op jit(solution)/shard_map/all_to_all | solution.py:627
  226.4 14.0 %all-to-all-done.1 = bf16[512,2,512]{2,0,1:T(8,128)(2,1)} async-done(((bf16[512,2,512]{2,0,1:T(8,128)(2,1)}), bf16[512,2,512]{2,0,1:T(8,128)(2,1)}, u32[]{:S(2)}, u32[]{:S(2)}) %all-to-all-start.1) | async-done | bytes 1048608 | tf_op jit(solution)/shard_map/all_to_all | solution.py:627
  240.4 25.1 %attend_backward.1 = (bf16[1024,512]{1,0:T(8,128)(2,1)}, bf16[1024,512]{1,0:T(8,128)(2,1)}, bf16[1024,512]{1,0:T(8,128)(2,1)}) custom-call(bf16[1024,512]{1,0:T(8,128)(2,1)} %get-tuple-element.22.q_ref, bf16[1024,512]{1,0:T(8,128)(2,1)} %get-tuple-element.23.k_ref, bf16[1024,512]{1,0:T(8,128)(2,1)} %get-tuple-element.24.v_ref, ...), custom_call_target="tpu_custom_call" | custom-call | flops 8053063680 | bytes 7340032 | tf_op jit(solution)/shard_map/attend_backward/pallas_call | solution.py:173
  265.5 13.1 %heads_backward.1 = bf16[1024,768]{1,0:T(8,128)(2,1)} custom-call(f32[1024,768]{1,0:T(8,128)} %get-tuple-element.28.f_ref, bf16[256,5120]{1,0:T(8,128)(2,1)} %fusion.13.e_ref, bf16[1024,512]{1,0:T(8,128)(2,1)} %get-tuple-element.30.dq_ref, bf16[1024,512]{1,0:T(8,128)(2,1)} %get-tuple-element.31.dk_ref, bf16[1024,512]{1,0:T(8,128)(2,1)} %get-tuple-element.32.dv_ref), custom_call_target="tpu_custom_call" | custom-call | tf_op jit(solution)/shard_map/heads_backward/pallas_call | solution.py:278
  278.6 5.0 %all-to-all-start.2 = ((bf16[2,512,768]{2,1,0:T(8,128)(2,1)}), bf16[2,512,768]{2,1,0:T(8,128)(2,1)}, u32[]{:S(2)}, u32[]{:S(2)}) async-start(bf16[2,512,768]{2,1,0:T(8,128)(2,1)} %bitcast.76), calls=%async_computation.2 | async-start | bytes 3145728 | tf_op jit(solution)/shard_map/all_to_all | solution.py:637
  283.6 7.8 %fusion.33 = bf16[1,512,1024]{2,1,0:T(8,128)(2,1)} fusion(f32[512,1024]{1,0:T(8,128)S(1)} %get-tuple-element.63, bf16[512,2816]{1,0:T(8,128)(2,1)} %copy-done.8, bf16[2816,1024]{1,0:T(8,128)(2,1)} %all-gather.5.cloned.1.call-done), kind=kOutput, calls=%fused_computation.65 | convolution fusion | flops 2953838592 | bytes 11796480 | tf_op jit(solution)/shard_map/dot_general | solution.py:37
  291.5 4.2 convolution_convert_fusion.3.out_ref
  295.7 3.9 convolution_convert_fusion.2.rest_ref
  305.0 4.2 fusion.18
  314.0 94.7 %scatter_packed.1 = f32[64,3072]{1,0:T(8,128)} custom-call(bf16[1024,896]{1,0:T(8,128)(2,1)} %convolution_convert_fusion.4.fac_ref, bf16[1024,1024]{1,0:T(8,128)(2,1)} %convolution_convert_fusion.3.out_ref, bf16[1024,1024]{1,0:T(8,128)(2,1)} %convolution_convert_fusion.2.rest_ref, bf16[16,64,128]{2,1,0:T(8,128)(2,1)} %pad.27.gains_ref), custom_call_target="tpu_custom_call" | custom-call | tf_op jit(solution)/shard_map/scatter_packed/pallas_call | solution.py:507
  410.4 4.9 %fusion.21 = f32[1,512,1024]{2,1,0:T(8,128)} fusion(f32[512,1024]{1,0:T(8,128)} %get-tuple-element.65, f32[512]{0:T(512)S(1)} %multiply_multiply_fusion.1, f32[512]{0:T(512)S(1)} %fusion.61, f32[1024]{0:T(1024)S(1)} %mul.201, bf16[1,512,1024]{2,1,0:T(8,128)(2,1)S(1)} %copy-done.2, f32[512,1024]{1,0:T(8,128)S(1)} %get-tuple-element.63, ...), kind=kLoop, calls=%fused_computation.47 | loop fusion | flops 7340032 | bytes 10502144 | tf_op jit(solution)/shard_map/reshape | solution.py:649
  421.2 5.5 %collective-permute-done.3 = bf16[176,1024]{1,0:T(8,128)(2,1)S(1)} collective-permute-done((bf16[176,1024]{1,0:T(8,128)(2,1)}, bf16[176,1024]{1,0:T(8,128)(2,1)S(1)}, u32[]{:S(2)}, u32[]{:S(2)}) %collective-permute-start.3) | collective-permute-done | bytes 360480 | tf_op jit(solution)/shard_map/ppermute | solution.py:538
  427.7 10.3 %collective-permute-done.2 = bf16[64,4608]{1,0:T(8,128)(2,1)S(1)} collective-permute-done((bf16[64,4608]{1,0:T(8,128)(2,1)}, bf16[64,4608]{1,0:T(8,128)(2,1)S(1)}, u32[]{:S(2)}, u32[]{:S(2)}) %collective-permute-start.2) | collective-permute-done | bytes 589856 | tf_op jit(solution)/shard_map/ppermute | solution.py:538
  (122 shorter events, 70.4 us)
Async XLA Ops:
  7.2 121.6 %all-gather.3.cloned.1.call-start = ((), (), s32[]{:S(2)}) async-start(), calls=%async_computation.5 | async-start | bytes 12255232 | tf_op jit(solution)/shard_map/all_gather | solution.py:579
  7.9 165.3 %all-gather.5.cloned.1.call-start = ((), (), s32[]{:S(2)}) async-start(), calls=%async_computation.6 | async-start | bytes 6127616 | tf_op jit(solution)/shard_map/all_gather | solution.py:580
  8.7 62.9 %collective-permute-start.1 = (s32[512]{0:T(512)}, s32[512]{0:T(512)S(1)}, u32[]{:S(2)}, u32[]{:S(2)}) collective-permute-start(s32[512]{0:T(512)} %bitcast.88), channel_id=1, source_target_pairs={{0,16},{16,0},{1,17},{17,1},{2,18},{18,2},{3,19},{19,3},{4,20},{20... | collective-permute-start | bytes 6152 | tf_op jit(solution)/shard_map/ppermute | solution.py:531
  10.2 62.5 %collective-permute-start = (bf16[512,1024]{1,0:T(8,128)(2,1)}, bf16[512,1024]{1,0:T(8,128)(2,1)}, u32[]{:S(2)}, u32[]{:S(2)}) collective-permute-start(bf16[512,1024]{1,0:T(8,128)(2,1)} %bitcast.75), channel_id=1, source_target_pairs={{0,16},{16,0},{1,17},{17,1},{2,18},{18,2},{3,19},{19,3},{4,20},{20... | collective-permute-start | bytes 3145736 | tf_op jit(solution)/shard_map/ppermute | solution.py:531
  66.6 2.8 copy-start.5
  71.7 14.4 %copy-start.17 = (s32[1024]{0:T(1024)}, s32[1024]{0:T(1024)S(1)}, u32[]{:S(2)}) copy-start(s32[1024]{0:T(1024)S(1)} %dynamic_update_slice.15) | copy-start | bytes 12292
  105.3 17.9 %all-to-all-start = ((bf16[2,512,512]{1,2,0:T(8,128)(2,1)}), bf16[2,512,512]{1,2,0:T(8,128)(2,1)S(1)}, u32[]{:S(2)}, u32[]{:S(2)}) async-start(bf16[2,512,512]{1,2,0:T(8,128)(2,1)} %copy.19), calls=%async_computation | async-start | bytes 2097152 | tf_op jit(solution)/shard_map/all_to_all | solution.py:597
  108.8 306.4 %reduce-scatter.5.cloned.1.call-start = ((), (), s32[]{:S(2)}) async-start(), calls=%async_computation.8 | async-start | bytes 6127616 | tf_op jit(solution)/shard_map/reduce_scatter | solution.py:609
  138.0 4.2 copy-start.1
  138.0 5.8 %copy-start.6 = (bf16[1,512,1024]{2,1,0:T(8,128)(2,1)S(1)}, bf16[1,512,1024]{2,1,0:T(8,128)(2,1)}, u32[]{:S(2)}) copy-start(bf16[1,512,1024]{2,1,0:T(8,128)(2,1)} %param.11) | copy-start | bytes 3145732
  148.8 267.4 %reduce-scatter.3.cloned.1.call-start = ((), (), s32[]{:S(2)}) async-start(), calls=%async_computation.7 | async-start | bytes 10027008 | tf_op jit(solution)/shard_map/reduce_scatter | solution.py:626
  193.7 11.7 %copy-start.7 = (bf16[1,512,1024]{2,1,0:T(8,128)(2,1)S(1)}, bf16[1,512,1024]{2,1,0:T(8,128)(2,1)}, u32[]{:S(2)}) copy-start(bf16[1,512,1024]{2,1,0:T(8,128)(2,1)} %param.11) | copy-start | bytes 3145732
  205.4 3.4 copy-start
  205.5 5.7 %slice-start = ((s8[5767168]{0:T(1024)(128)(4,1)}), s8[4194304]{0:T(1024)(128)(4,1)S(1)}, s32[]{:S(2)}) async-start(s8[5767168]{0:T(1024)(128)(4,1)} %bitcast.77), calls=%async_computation.9 | async-start | bytes 8388608
  208.9 2.6 copy-start.10
  221.5 19.0 %all-to-all-start.1 = ((bf16[512,2,512]{2,0,1:T(8,128)(2,1)}), bf16[512,2,512]{2,0,1:T(8,128)(2,1)}, u32[]{:S(2)}, u32[]{:S(2)}) async-start(bf16[512,2,512]{2,0,1:T(8,128)(2,1)} %bitcast.79), calls=%async_computation.1 | async-start | bytes 2097152 | tf_op jit(solution)/shard_map/all_to_all | solution.py:627
  278.6 23.6 %all-to-all-start.2 = ((bf16[2,512,768]{2,1,0:T(8,128)(2,1)}), bf16[2,512,768]{2,1,0:T(8,128)(2,1)}, u32[]{:S(2)}, u32[]{:S(2)}) async-start(bf16[2,512,768]{2,1,0:T(8,128)(2,1)} %bitcast.76), calls=%async_computation.2 | async-start | bytes 3145728 | tf_op jit(solution)/shard_map/all_to_all | solution.py:637
  291.5 4.2 copy-start.11
  303.7 5.5 %copy-start.13 = (bf16[512,640]{1,0:T(8,128)(2,1)}, bf16[512,640]{1,0:T(8,128)(2,1)S(1)}, u32[]{:S(2)}) copy-start(bf16[512,640]{1,0:T(8,128)(2,1)S(1)} %slice_reduce_fusion) | copy-start | bytes 1966084
  410.4 8.3 %slice-start.2 = ((f32[64,3072]{1,0:T(8,128)}), f32[64,640]{1,0:T(8,128)S(1)}, s32[]{:S(2)}) async-start(f32[64,3072]{1,0:T(8,128)} %scatter_packed.1), calls=%async_computation.11 | async-start | bytes 327680 | tf_op jit(solution)/shard_map/slice | solution.py:563
  415.3 11.5 %copy-start.16 = (bf16[176,1024]{1,0:T(8,128)(2,1)S(1)}, bf16[176,1024]{1,0:T(8,128)(2,1)}, u32[]{:S(2)}) copy-start(bf16[176,1024]{1,0:T(8,128)(2,1)} %reduce-scatter.5.cloned.1.call-done) | copy-start | bytes 1081348
  415.3 11.5 %collective-permute-start.3 = (bf16[176,1024]{1,0:T(8,128)(2,1)}, bf16[176,1024]{1,0:T(8,128)(2,1)S(1)}, u32[]{:S(2)}, u32[]{:S(2)}) collective-permute-start(bf16[176,1024]{1,0:T(8,128)(2,1)} %reduce-scatter.5.cloned.1.call-done), channel_id=1, source_target_pairs={{0,16},{16,0},{1,17},{17,1},{2,18},{18,2},{3,19},{19,3},{4,20},{20... | collective-permute-start | bytes 1081352 | tf_op jit(solution)/shard_map/ppermute | solution.py:538
  416.2 21.8 %copy-start.14 = (bf16[64,4608]{1,0:T(8,128)(2,1)S(1)}, bf16[64,4608]{1,0:T(8,128)(2,1)}, u32[]{:S(2)}) copy-start(bf16[64,4608]{1,0:T(8,128)(2,1)} %reduce-scatter.3.cloned.1.call-done) | copy-start | bytes 1769476
  416.2 21.8 %collective-permute-start.2 = (bf16[64,4608]{1,0:T(8,128)(2,1)}, bf16[64,4608]{1,0:T(8,128)(2,1)S(1)}, u32[]{:S(2)}, u32[]{:S(2)}) collective-permute-start(bf16[64,4608]{1,0:T(8,128)(2,1)} %reduce-scatter.3.cloned.1.call-done), channel_id=1, source_target_pairs={{0,16},{16,0},{1,17},{17,1},{2,18},{18,2},{3,19},{19,3},{4,20},{20... | collective-permute-start | bytes 1769480 | tf_op jit(solution)/shard_map/ppermute | solution.py:538
  (9 other events, 13.0 us)
Sparse Core Ops, SparseCore 0:
  10.3 102.8 all-gather.2
  115.4 57.8 all-gather.4
  177.1 80.6 reduce-scatter.4
  261.8 135.7 reduce-scatter.2
where the time goes:
time: 452 us; the launch traced here: 446 us
  Pallas kernels  205 us (45%)
  matrix products  75.5 us (17%)
  waiting for transfers between devices  71.6 us (16%)
  local copies, waits for them, and re-layouts  34.7 us (8%)
  other arithmetic  26.6 us (6%)
  starting transfers between devices  18.2 us (4%)
  between operations  14.3 us (3%)
    pallas_call x1, Pallas kernels, scatter_packed(): pl.pallas_call(functools.partial(scatter_kernel, count=count, shards=shar...  94.7 us
    pallas_call x1, Pallas kernels, gather_packed(): pl.pallas_call(functools.partial(gather_kernel, count=count, split=split)...  44.7 us
    dot_general x4, matrix products, back_product(): jnp.einsum('tb,ab->ta', grad_rows, weight, preferred_element_type=F32)  30.5 us
    pallas_call x1, Pallas kernels, attend_backward(): pl.pallas_call(functools.partial(attend_backward_kernel, block=block, wid...  25.1 us
    dot_general x5, matrix products, weight_grad(): return jnp.einsum('ta,tb->ab', left, right, preferred_element_type=F32)  24.5 us
    all_gather x1, waiting for transfers between devices, local(): down_full = lax.all_gather(w_down, 'fsdp', axis=0, tiled=True)  23.9 us
    dot_general x3, matrix products, product(): return jnp.dot(left, right, preferred_element_type=F32)  20.4 us
    pallas_call x1, Pallas kernels, attend_forward(): pl.pallas_call(functools.partial(attend_forward_kernel, block=block, widt...  16.9 us
  transfers between devices with their start and end apart: 11, of which 6 were waited for; matrix products, arithmetic and copies ran while one was open for 28% of the time, Pallas kernels for 46%

commit v1 on v0

--- a/solution.py
+++ b/solution.py
@@ -16,7 +16,7 @@
 LANES = 128
 NB = (RQ + 2 * RK) * DH
 RANKS = RQ + 2 * RK
-MOVED = 1024
+MOVED = 1280
 
 EPSILON = 1e-06
 NEG = -1e30
@@ -394,9 +394,8 @@
 
 
 def scatter_kernel(
-    fac_ref, out_ref, rest_ref, gains_ref, o_ref, part, core_in, side_in, line_in, mine, sp_in, last_in,
+    fac_ref, out_ref, rest_ref, gains_ref, o_ref, part, core_in, side_in, line_in, mine, sp_in,
     core_send, core_recv, side_send, side_recv, line_send, line_recv, sp_send, sp_recv,
-    last_send, last_recv,
     *, count, shards
 ):
     me, line, side, core, lines = place(count)
@@ -451,45 +450,23 @@
         shard = spot(target, side, core)
         return load(shard).astype(F32) + from_core(target * 2 + side) + from_side(target)
 
-    if shards == 2:
-        mate, span, rest = halves(o_ref.shape[1])
-        for s, target in enumerate(targets):
+    for s, target in enumerate(targets):
+        total = whole_sum(target)
+        if s < lines - 1:
             shard = spot(target, side, core)
-            part[shard] = whole_sum(target).astype(BF16)
-            send(part.at[shard, :, rest], sp_in.at[s], sp_send.at[s], sp_recv.at[s], mate)
-        for s, target in enumerate(targets):
-            shard = spot(target, side, core)
-            copy(part.at[me, :, rest], sp_in.at[s], sp_send.at[s], sp_recv.at[s], mate).wait_recv()
-            total = part[shard, :, span].astype(F32) + sp_in[s].astype(F32)
-            if s < lines - 1:
-                mine[s] = total.astype(BF16)
-                send(mine.at[s], line_in.at[s], line_send.at[s], line_recv.at[s], across[s])
-        for s in range(lines - 1):
-            copy(mine.at[s], line_in.at[s], line_send.at[s], line_recv.at[s], across[s]).wait_recv()
-            total = total + line_in[s].astype(F32)
-        mine[lines - 1] = total.astype(BF16)
-        send(mine.at[lines - 1], last_in, last_send, last_recv, mate)
-        o_ref[:, span] = mine[lines - 1].astype(F32)
-        copy(mine.at[lines - 1], last_in, last_send, last_recv, mate).wait_recv()
-        o_ref[:, rest] = last_in[...].astype(F32)
-    else:
-        for s, target in enumerate(targets):
-            total = whole_sum(target)
-            if s < lines - 1:
-                shard = spot(target, side, core)
-                part[shard] = total.astype(BF16)
-                send(part.at[shard], line_in.at[s], line_send.at[s], line_recv.at[s], across[s])
-        for s in range(lines - 1):
-            copy(part.at[me], line_in.at[s], line_send.at[s], line_recv.at[s], across[s]).wait_recv()
-            total = total + line_in[s].astype(F32)
-        mine[0] = total.astype(BF16)
-        for s, peer in enumerate(others):
-            send(mine.at[0], sp_in.at[s], sp_send.at[s], sp_recv.at[s], peer)
-        total = mine[0].astype(F32)
-        for s, peer in enumerate(others):
-            copy(mine.at[0], sp_in.at[s], sp_send.at[s], sp_recv.at[s], peer).wait_recv()
-            total = total + sp_in[s].astype(F32)
-        o_ref[...] = total
+            part[shard] = total.astype(BF16)
+            send(part.at[shard], line_in.at[s], line_send.at[s], line_recv.at[s], across[s])
+    for s in range(lines - 1):
+        copy(part.at[me], line_in.at[s], line_send.at[s], line_recv.at[s], across[s]).wait_recv()
+        total = total + line_in[s].astype(F32)
+    mine[0] = total.astype(BF16)
+    for s, peer in enumerate(others):
+        send(mine.at[0], sp_in.at[s], sp_send.at[s], sp_recv.at[s], peer)
+    total = mine[0].astype(F32)
+    for s, peer in enumerate(others):
+        copy(mine.at[0], sp_in.at[s], sp_send.at[s], sp_recv.at[s], peer).wait_recv()
+        total = total + sp_in[s].astype(F32)
+    o_ref[...] = total
     for made in started:
         made.wait_send()
 
@@ -498,11 +475,7 @@
     rows = grad_fac.shape[0] // count
     columns = sum(a.shape[-1] for a in (grad_fac, grad_out, grad_rest, grad_gains))
     lines = count // 4
-    split = shards == 2
-    span = columns // 2 if split else columns
-    passes = lines if split else shards - 1
     buffer = lambda n: pltpu.VMEM((n, rows, columns), BF16)
-    narrow = lambda n: pltpu.VMEM((n, rows, span), BF16)
     sems = lambda n: pltpu.SemaphoreType.DMA((n,))
     return pl.pallas_call(
         functools.partial(scatter_kernel, count=count, shards=shards),
@@ -510,11 +483,10 @@
         in_specs=[pl.BlockSpec(memory_space=pltpu.VMEM)] * 4,
         out_specs=pl.BlockSpec(memory_space=pltpu.VMEM),
         scratch_shapes=[
-            buffer(count), buffer(2 * lines), buffer(lines), narrow(lines - 1),
-            narrow(lines if split else 1), narrow(passes), pltpu.VMEM((rows, span), BF16),
+            buffer(count), buffer(2 * lines), buffer(lines), buffer(lines - 1),
+            buffer(1), buffer(shards - 1),
             sems(2 * lines), sems(2 * lines), sems(lines), sems(lines),
-            sems(lines - 1), sems(lines - 1), sems(passes), sems(passes),
-            pltpu.SemaphoreType.DMA, pltpu.SemaphoreType.DMA,
+            sems(lines - 1), sems(lines - 1), sems(shards - 1), sems(shards - 1),
         ],
         compiler_params=pltpu.CompilerParams(collective_id=1, has_side_effects=True),
         name="scatter_packed",

time: 452 us -> 454 us (level)
  the two profiles are of different devices: /device:TPU:12 before, /device:TPU:0 now
where the time goes in v1:
time: 454 us; the launch traced here: 447 us
  Pallas kernels  206 us (45%)
  matrix products  75.3 us (17%)
  waiting for transfers between devices  71.6 us (16%)
  local copies, waits for them, and re-layouts  34 us (7%)
  other arithmetic  27.5 us (6%)
  starting transfers between devices  19.2 us (4%)
  between operations  14.3 us (3%)
    pallas_call x1, Pallas kernels, scatter_packed(): pl.pallas_call(functools.partial(scatter_kernel, count=count, shards=shar...  96 us
    pallas_call x1, Pallas kernels, gather_packed(): pl.pallas_call(functools.partial(gather_kernel, count=count, split=split)...  44 us
    dot_general x4, matrix products, back_product(): jnp.einsum('tb,ab->ta', grad_rows, weight, preferred_element_type=F32)  30.3 us
    all_gather x1, waiting for transfers between devices, local(): down_full = lax.all_gather(w_down, 'fsdp', axis=0, tiled=True)  26.3 us
    pallas_call x1, Pallas kernels, attend_backward(): pl.pallas_call(functools.partial(attend_backward_kernel, block=block, wid...  25 us
    dot_general x5, matrix products, weight_grad(): return jnp.einsum('ta,tb->ab', left, right, preferred_element_type=F32)  24.5 us
    dot_general x3, matrix products, product(): return jnp.dot(left, right, preferred_element_type=F32)  20.4 us
    pallas_call x1, Pallas kernels, attend_forward(): pl.pallas_call(functools.partial(attend_forward_kernel, block=block, widt...  16.8 us
  transfers between devices with their start and end apart: 11, of which 6 were waited for; matrix products, arithmetic and copies ran while one was open for 28% of the time, Pallas kernels for 46%

profile of v1, /device:TPU:0, one launch (start us, length us, event | category | flops | bytes accessed | tf_op | source)
XLA Modules:
  0.0 447.5 jit_solution(12701701910461138202)
XLA Ops:
  17.1 44.0 %gather_packed.1 = bf16[16,64,2048]{2,1,0:T(8,128)(2,1)} custom-call(bf16[64,2048]{1,0:T(8,128)(2,1)} %copy-done.15), custom_call_target="tpu_custom_call" | custom-call | tf_op jit(solution)/shard_map/gather_packed/pallas_call | solution.py:382
  75.4 10.7 %heads_forward.1 = (f32[1024,768]{1,0:T(8,128)}, bf16[1024,512]{1,0:T(8,128)(2,1)}, bf16[1024,512]{1,0:T(8,128)(2,1)}, bf16[1024,512]{1,0:T(8,128)(2,1)}) custom-call(bf16[1024,1024]{1,0:T(8,128)(2,1)} %copy-done.4, f32[1,1024]{1,0:T(1,128)} %reshape.89.gain_ref, bf16[1024,768]{1,0:T(8,128)(2,1)} %pad_maximum_fusion.w_ref, bf16[256,5120]{1,0:T(8,128)(2,1)} %fusion.13.e_ref), custom_call_target="tpu_custom_call" | custom-call | tf_op jit(solution)/shard_map/heads_forward/pallas_call | solution.py:264
  86.1 16.8 %attend_forward.1 = bf16[1024,512]{1,0:T(8,128)(2,1)} custom-call(bf16[1024,512]{1,0:T(8,128)(2,1)} %get-tuple-element.22.q_ref, bf16[1024,512]{1,0:T(8,128)(2,1)} %get-tuple-element.23.k_ref, bf16[1024,512]{1,0:T(8,128)(2,1)} %get-tuple-element.24.v_ref, s32[1024,1]{1,0:T(8,128)} %copy.18.segc_ref, s32[1,1024]{1,0:T(1,128)} %bitcast.86), custom_call_target="tpu_custom_call" | custom-call | flops 3221225472 | bytes 4194304 | tf_op jit(solution)/shard_map/attend_forward/pallas_call | solution.py:155
  109.2 13.9 %all-to-all-done = bf16[2,512,512]{1,2,0:T(8,128)(2,1)S(1)} async-done(((bf16[2,512,512]{1,2,0:T(8,128)(2,1)}), bf16[2,512,512]{1,2,0:T(8,128)(2,1)S(1)}, u32[]{:S(2)}, u32[]{:S(2)}) %all-to-all-start) | async-done | bytes 1048608 | tf_op jit(solution)/shard_map/all_to_all | solution.py:569
  128.7 9.3 %fusion.73 = f32[512,5632]{1,0:T(8,128)S(1)} fusion(bf16[512,1024]{1,0:T(8,128)(2,1)} %multiply_convert_fusion, bf16[1024,5632]{1,0:T(8,128)(2,1)} %all-gather.3.cloned.1.call-done), kind=kOutput, calls=%fused_computation.133 | convolution fusion | flops 5905580032 | bytes 24117248 | tf_op jit(solution)/shard_map/dot_general | solution.py:37
  143.8 5.0 %convolution_convert_fusion.1 = bf16[2816,1024]{1,0:T(8,128)(2,1)} fusion(bf16[512,2816]{1,0:T(8,128)(2,1)S(1)} %fusion.2, bf16[1,512,1024]{2,1,0:T(8,128)(2,1)S(1)} %copy-done.6), kind=kOutput, calls=%fused_computation.21 | convolution fusion | flops 2955673600 | bytes 9699328 | tf_op jit(solution)/shard_map/ta,tb->ab/dot_general | solution.py:41
  149.4 26.3 %all-gather.5.cloned.1.call-done = bf16[2816,1024]{1,0:T(8,128)(2,1)} async-done(((bf16[176,1024]{1,0:T(8,128)(2,1)}), bf16[2816,1024]{1,0:T(8,128)(2,1)}) %all-gather.5.cloned.1.call-update) | async-done | bytes 5767184 | tf_op jit(solution)/shard_map/all_gather | solution.py:552
  175.7 12.3 %multiply_multiply_fusion = (f32[512,2816]{1,0:T(8,128)}, f32[512,2816]{1,0:T(8,128)}) fusion(f32[512,5632]{1,0:T(8,128)} %copy-done.1, bf16[2816,1024]{1,0:T(8,128)(2,1)} %all-gather.5.cloned.1.call-done, bf16[1,512,1024]{2,1,0:T(8,128)(2,1)} %param.11), kind=kOutput, calls=%fused_computation.19 | convolution fusion | flops 2970091520 | bytes 29884416 | tf_op jit(solution)/shard_map/tb,ab->ta/dot_general | solution.py:45
  188.0 8.2 %add_convert_fusion = bf16[512,5632]{1,0:T(8,128)(2,1)} fusion(f32[512,2816]{1,0:T(8,128)} %get-tuple-element.41, f32[512,2816]{1,0:T(8,128)} %get-tuple-element.40), kind=kLoop, calls=%fused_computation.9 | loop fusion | flops 5767168 | bytes 17301504 | tf_op jit(solution)/shard_map/convert_element_type | solution.py:588
  196.2 11.5 %multiply_reduce_fusion = (bf16[1024]{0:T(1024)(128)(2,1)S(1)}, f32[512]{0:T(512)S(1)}, f32[512,1024]{1,0:T(8,128)S(1)}) fusion(f32[512,1024]{1,0:T(8,128)S(1)} %get-tuple-element.61, f32[512]{0:T(512)S(1)} %fusion.60, f32[1024]{0:T(1024)S(1)} %mul.183, bf16[512,5632]{1,0:T(8,128)(2,1)} %add_convert_fusion, bf16[1024,5632]{1,0:T(8,128)(2,1)} %all-gather.3.cloned.1.call-done), kind=kOutput, calls=%fused_computation.51 | convolution fusion | flops 5908724224 | bytes 21506048 | tf_op jit(solution)/shard_map/tb,ab->ta/dot_general | solution.py:45
  213.4 7.1 %convolution_convert_fusion = bf16[1024,4352]{1,0:T(8,128)(2,1)} fusion(bf16[512,1024]{1,0:T(8,128)(2,1)S(1)} %copy-done.10, bf16[512,5632]{1,0:T(8,128)(2,1)S(1)} %bitcast.78), kind=kOutput, calls=%fused_computation.10 | convolution fusion | flops 4567859200 | bytes 14417920 | tf_op jit(solution)/shard_map/ta,tb->ab/dot_general | solution.py:41
  222.8 4.6 %all-to-all-start.1 = ((bf16[512,2,512]{2,0,1:T(8,128)(2,1)}), bf16[512,2,512]{2,0,1:T(8,128)(2,1)}, u32[]{:S(2)}, u32[]{:S(2)}) async-start(bf16[512,2,512]{2,0,1:T(8,128)(2,1)} %bitcast.79), calls=%async_computation.1 | async-start | bytes 2097152 | tf_op jit(solution)/shard_map/all_to_all | solution.py:599
  227.8 14.0 %all-to-all-done.1 = bf16[512,2,512]{2,0,1:T(8,128)(2,1)} async-done(((bf16[512,2,512]{2,0,1:T(8,128)(2,1)}), bf16[512,2,512]{2,0,1:T(8,128)(2,1)}, u32[]{:S(2)}, u32[]{:S(2)}) %all-to-all-start.1) | async-done | bytes 1048608 | tf_op jit(solution)/shard_map/all_to_all | solution.py:599
  241.8 25.0 %attend_backward.1 = (bf16[1024,512]{1,0:T(8,128)(2,1)}, bf16[1024,512]{1,0:T(8,128)(2,1)}, bf16[1024,512]{1,0:T(8,128)(2,1)}) custom-call(bf16[1024,512]{1,0:T(8,128)(2,1)} %get-tuple-element.22.q_ref, bf16[1024,512]{1,0:T(8,128)(2,1)} %get-tuple-element.23.k_ref, bf16[1024,512]{1,0:T(8,128)(2,1)} %get-tuple-element.24.v_ref, ...), custom_call_target="tpu_custom_call" | custom-call | flops 8053063680 | bytes 7340032 | tf_op jit(solution)/shard_map/attend_backward/pallas_call | solution.py:173
  266.8 13.1 %heads_backward.1 = bf16[1024,768]{1,0:T(8,128)(2,1)} custom-call(f32[1024,768]{1,0:T(8,128)} %get-tuple-element.28.f_ref, bf16[256,5120]{1,0:T(8,128)(2,1)} %fusion.13.e_ref, bf16[1024,512]{1,0:T(8,128)(2,1)} %get-tuple-element.30.dq_ref, bf16[1024,512]{1,0:T(8,128)(2,1)} %get-tuple-element.31.dk_ref, bf16[1024,512]{1,0:T(8,128)(2,1)} %get-tuple-element.32.dv_ref), custom_call_target="tpu_custom_call" | custom-call | tf_op jit(solution)/shard_map/heads_backward/pallas_call | solution.py:278
  279.9 4.9 %all-to-all-start.2 = ((bf16[2,512,768]{2,1,0:T(8,128)(2,1)}), bf16[2,512,768]{2,1,0:T(8,128)(2,1)}, u32[]{:S(2)}, u32[]{:S(2)}) async-start(bf16[2,512,768]{2,1,0:T(8,128)(2,1)} %bitcast.76), calls=%async_computation.2 | async-start | bytes 3145728 | tf_op jit(solution)/shard_map/all_to_all | solution.py:609
  284.8 7.8 %fusion.33 = bf16[1,512,1024]{2,1,0:T(8,128)(2,1)} fusion(f32[512,1024]{1,0:T(8,128)S(1)} %get-tuple-element.61, bf16[512,2816]{1,0:T(8,128)(2,1)} %copy-done.8, bf16[2816,1024]{1,0:T(8,128)(2,1)} %all-gather.5.cloned.1.call-done), kind=kOutput, calls=%fused_computation.65 | convolution fusion | flops 2953838592 | bytes 11796480 | tf_op jit(solution)/shard_map/dot_general | solution.py:37
  292.7 4.2 convolution_convert_fusion.3.out_ref
  296.9 4.4 convolution_convert_fusion.2.rest_ref
  306.5 4.2 fusion.18
  315.5 96.0 %scatter_packed.1 = f32[64,3328]{1,0:T(8,128)} custom-call(bf16[1024,896]{1,0:T(8,128)(2,1)} %convolution_convert_fusion.4.fac_ref, bf16[1024,1024]{1,0:T(8,128)(2,1)} %convolution_convert_fusion.3.out_ref, bf16[1024,1280]{1,0:T(8,128)(2,1)} %convolution_convert_fusion.2.rest_ref, bf16[16,64,128]{2,1,0:T(8,128)(2,1)} %pad.27.gains_ref), custom_call_target="tpu_custom_call" | custom-call | tf_op jit(solution)/shard_map/scatter_packed/pallas_call | solution.py:480
  412.4 4.9 %fusion.21 = f32[1,512,1024]{2,1,0:T(8,128)} fusion(f32[512,1024]{1,0:T(8,128)} %get-tuple-element.63, f32[512]{0:T(512)S(1)} %multiply_multiply_fusion.1, f32[512]{0:T(512)S(1)} %fusion.61, f32[1024]{0:T(1024)S(1)} %mul.201, bf16[1,512,1024]{2,1,0:T(8,128)(2,1)S(1)} %copy-done.2, f32[512,1024]{1,0:T(8,128)S(1)} %get-tuple-element.61, ...), kind=kLoop, calls=%fused_computation.48 | loop fusion | flops 7340032 | bytes 10502144 | tf_op jit(solution)/shard_map/reshape | solution.py:621
  424.0 4.8 %collective-permute-done.3 = bf16[176,1024]{1,0:T(8,128)(2,1)S(1)} collective-permute-done((bf16[176,1024]{1,0:T(8,128)(2,1)}, bf16[176,1024]{1,0:T(8,128)(2,1)S(1)}, u32[]{:S(2)}, u32[]{:S(2)}) %collective-permute-start.3) | collective-permute-done | bytes 360480 | tf_op jit(solution)/shard_map/ppermute | solution.py:510
  430.7 8.7 %collective-permute-done.2 = bf16[64,4352]{1,0:T(8,128)(2,1)S(1)} collective-permute-done((bf16[64,4352]{1,0:T(8,128)(2,1)}, bf16[64,4352]{1,0:T(8,128)(2,1)S(1)}, u32[]{:S(2)}, u32[]{:S(2)}) %collective-permute-start.2) | collective-permute-done | bytes 557088 | tf_op jit(solution)/shard_map/ppermute | solution.py:510
  (122 shorter events, 71.5 us)
Async XLA Ops:
  7.2 121.6 %all-gather.3.cloned.1.call-start = ((), (), s32[]{:S(2)}) async-start(), calls=%async_computation.5 | async-start | bytes 12255232 | tf_op jit(solution)/shard_map/all_gather | solution.py:551
  7.9 167.8 %all-gather.5.cloned.1.call-start = ((), (), s32[]{:S(2)}) async-start(), calls=%async_computation.6 | async-start | bytes 6127616 | tf_op jit(solution)/shard_map/all_gather | solution.py:552
  8.7 62.9 %collective-permute-start.1 = (s32[512]{0:T(512)}, s32[512]{0:T(512)S(1)}, u32[]{:S(2)}, u32[]{:S(2)}) collective-permute-start(s32[512]{0:T(512)} %bitcast.88), channel_id=1, source_target_pairs={{0,16},{16,0},{1,17},{17,1},{2,18},{18,2},{3,19},{19,3},{4,20},{20... | collective-permute-start | bytes 6152 | tf_op jit(solution)/shard_map/ppermute | solution.py:503
  11.7 61.1 %collective-permute-start = (bf16[512,1024]{1,0:T(8,128)(2,1)}, bf16[512,1024]{1,0:T(8,128)(2,1)}, u32[]{:S(2)}, u32[]{:S(2)}) collective-permute-start(bf16[512,1024]{1,0:T(8,128)(2,1)} %bitcast.75), channel_id=1, source_target_pairs={{0,16},{16,0},{1,17},{17,1},{2,18},{18,2},{3,19},{19,3},{4,20},{20... | collective-permute-start | bytes 3145736 | tf_op jit(solution)/shard_map/ppermute | solution.py:503
  63.6 3.0 copy-start.2
  66.7 4.0 copy-start.17
  71.7 14.4 %copy-start.16 = (s32[1024]{0:T(1024)}, s32[1024]{0:T(1024)S(1)}, u32[]{:S(2)}) copy-start(s32[1024]{0:T(1024)S(1)} %dynamic_update_slice.15) | copy-start | bytes 12292
  105.2 17.9 %all-to-all-start = ((bf16[2,512,512]{1,2,0:T(8,128)(2,1)}), bf16[2,512,512]{1,2,0:T(8,128)(2,1)S(1)}, u32[]{:S(2)}, u32[]{:S(2)}) async-start(bf16[2,512,512]{1,2,0:T(8,128)(2,1)} %copy.19), calls=%async_computation | async-start | bytes 2097152 | tf_op jit(solution)/shard_map/all_to_all | solution.py:569
  108.8 308.5 %reduce-scatter.5.cloned.1.call-start = ((), (), s32[]{:S(2)}) async-start(), calls=%async_computation.8 | async-start | bytes 6127616 | tf_op jit(solution)/shard_map/reduce_scatter | solution.py:581
  138.0 4.2 copy-start.1
  138.0 5.8 %copy-start.6 = (bf16[1,512,1024]{2,1,0:T(8,128)(2,1)S(1)}, bf16[1,512,1024]{2,1,0:T(8,128)(2,1)}, u32[]{:S(2)}) copy-start(bf16[1,512,1024]{2,1,0:T(8,128)(2,1)} %param.11) | copy-start | bytes 3145732
  148.8 269.6 %reduce-scatter.3.cloned.1.call-start = ((), (), s32[]{:S(2)}) async-start(), calls=%async_computation.7 | async-start | bytes 9469952 | tf_op jit(solution)/shard_map/reduce_scatter | solution.py:598
  196.2 11.5 %copy-start.7 = (bf16[1,512,1024]{2,1,0:T(8,128)(2,1)S(1)}, bf16[1,512,1024]{2,1,0:T(8,128)(2,1)}, u32[]{:S(2)}) copy-start(bf16[1,512,1024]{2,1,0:T(8,128)(2,1)} %param.11) | copy-start | bytes 3145732
  207.7 3.0 copy-start
  207.8 5.3 %slice-start = ((s8[5767168]{0:T(1024)(128)(4,1)}), s8[4194304]{0:T(1024)(128)(4,1)S(1)}, s32[]{:S(2)}) async-start(s8[5767168]{0:T(1024)(128)(4,1)} %bitcast.77), calls=%async_computation.9 | async-start | bytes 8388608
  222.8 19.0 %all-to-all-start.1 = ((bf16[512,2,512]{2,0,1:T(8,128)(2,1)}), bf16[512,2,512]{2,0,1:T(8,128)(2,1)}, u32[]{:S(2)}, u32[]{:S(2)}) async-start(bf16[512,2,512]{2,0,1:T(8,128)(2,1)} %bitcast.79), calls=%async_computation.1 | async-start | bytes 2097152 | tf_op jit(solution)/shard_map/all_to_all | solution.py:599
  279.9 23.8 %all-to-all-start.2 = ((bf16[2,512,768]{2,1,0:T(8,128)(2,1)}), bf16[2,512,768]{2,1,0:T(8,128)(2,1)}, u32[]{:S(2)}, u32[]{:S(2)}) async-start(bf16[2,512,768]{2,1,0:T(8,128)(2,1)} %bitcast.76), calls=%async_computation.2 | async-start | bytes 3145728 | tf_op jit(solution)/shard_map/all_to_all | solution.py:609
  292.7 4.2 copy-start.11
  305.2 5.5 %copy-start.13 = (bf16[512,640]{1,0:T(8,128)(2,1)}, bf16[512,640]{1,0:T(8,128)(2,1)S(1)}, u32[]{:S(2)}) copy-start(bf16[512,640]{1,0:T(8,128)(2,1)S(1)} %slice_reduce_fusion) | copy-start | bytes 1966084
  412.4 9.4 %slice-start.2 = ((f32[64,3328]{1,0:T(8,128)}), f32[64,640]{1,0:T(8,128)S(1)}, s32[]{:S(2)}) async-start(f32[64,3328]{1,0:T(8,128)} %scatter_packed.1), calls=%async_computation.11 | async-start | bytes 327680 | tf_op jit(solution)/shard_map/slice | solution.py:535
  417.3 11.5 %collective-permute-start.3 = (bf16[176,1024]{1,0:T(8,128)(2,1)}, bf16[176,1024]{1,0:T(8,128)(2,1)S(1)}, u32[]{:S(2)}, u32[]{:S(2)}) collective-permute-start(bf16[176,1024]{1,0:T(8,128)(2,1)} %reduce-scatter.5.cloned.1.call-done), channel_id=1, source_target_pairs={{0,16},{16,0},{1,17},{17,1},{2,18},{18,2},{3,19},{19,3},{4,20},{20... | collective-permute-start | bytes 1081352 | tf_op jit(solution)/shard_map/ppermute | solution.py:510
  418.4 21.0 %copy-start.14 = (bf16[64,4352]{1,0:T(8,128)(2,1)S(1)}, bf16[64,4352]{1,0:T(8,128)(2,1)}, u32[]{:S(2)}) copy-start(bf16[64,4352]{1,0:T(8,128)(2,1)} %reduce-scatter.3.cloned.1.call-done) | copy-start | bytes 1671172
  418.4 21.0 %collective-permute-start.2 = (bf16[64,4352]{1,0:T(8,128)(2,1)}, bf16[64,4352]{1,0:T(8,128)(2,1)S(1)}, u32[]{:S(2)}, u32[]{:S(2)}) collective-permute-start(bf16[64,4352]{1,0:T(8,128)(2,1)} %reduce-scatter.3.cloned.1.call-done), channel_id=1, source_target_pairs={{0,16},{16,0},{1,17},{17,1},{2,18},{18,2},{3,19},{19,3},{4,20},{20... | collective-permute-start | bytes 1671176 | tf_op jit(solution)/shard_map/ppermute | solution.py:510
  420.1 19.4 %slice-start.3 = ((f32[64,3328]{1,0:T(8,128)}), f32[64,1280]{1,0:T(8,128)S(1)}, s32[]{:S(2)}) async-start(f32[64,3328]{1,0:T(8,128)} %scatter_packed.1), calls=%async_computation.12 | async-start | bytes 655360 | tf_op jit(solution)/shard_map/slice | solution.py:637
  (9 other events, 15.9 us)
Sparse Core Ops, SparseCore 0:
  10.3 106.3 all-gather.2
  118.9 56.7 all-gather.4
  179.6 80.0 reduce-scatter.4
  263.7 135.2 reduce-scatter.2
